TPU v7x, 256 devices: a whole 4x4x8 slice. The times are simulated.
256 devices in a mesh: seq: 16 (over z, core), ch: 16 (over y, x).
Axes of the slice: x: 4, y: 4, z: 8, core: 2. Of those that a mesh axis runs over, the one named last changes fastest.
Arguments:
- query: bfloat16 [2048, 8192], P('seq', 'ch'), may hold values from -6 to 6
- key: bfloat16 [2048, 8192], P('seq', 'ch'), may hold values from -6 to 6
- value: bfloat16 [2048, 8192], P('seq', 'ch'), may hold values from -6 to 6
- short_taps: float32 [3, 3, 8192], P(None, None, 'ch'), may hold values from -3 to 3
- decay_rate: float32 [16, 8192], P(None, 'ch'), may hold values from 0.00012207031 to 0.05
- residue: float32 [16, 8192], P(None, 'ch'), may hold values from -2 to 2
- skip_gain: float32 [8192], P('ch'), may hold values from -4 to 4
- out_weight: bfloat16 [8192, 8192], P('ch', 'seq'), may hold values from -0.09375 to 0.09375
- grad_out: bfloat16 [2048, 8192], P('seq', 'ch'), may hold values from -6 to 6
Outputs:
- mixed: bfloat16 [2048, 8192], P('seq', 'ch')
- grad_query: bfloat16 [2048, 8192], P('seq', 'ch')
- grad_key: bfloat16 [2048, 8192], P('seq', 'ch')
- grad_value: bfloat16 [2048, 8192], P('seq', 'ch')
All inputs are finite; a program needn't handle non-finite values.
Results may differ from a plain program's by a relative error of at most 0.017.
Values may be sent and summed in bfloat16 or wider, within the bound.
A program may use at most 128 MiB of HBM per device.

v0:
```python
import jax
import jax.numpy as jnp
from jax import lax
from jax.sharding import PartitionSpec as P


def from_behind(block, axis, distance):
    devices = range(lax.axis_size(axis))
    route = [(i - distance, i) for i in devices if i - distance in devices]
    return lax.ppermute(block, axis, route)


def per_device(query, key, value, short_taps, decay_rate, residue, skip_gain, out_weight, grad_out):
    tok_rows, chan_width = query.shape
    tap_count = short_taps.shape[0]
    mode_count = decay_rate.shape[0]
    highest = lax.Precision.HIGHEST
    count = lax.axis_size("seq")
    place = lax.axis_index("seq")
    columns = lax.all_gather(out_weight, "seq", axis=1, tiled=True)
    grad_full = lax.all_gather(grad_out, "ch", axis=1, tiled=True)
    streams = jnp.stack([query, key, value])
    before = from_behind(streams[:, tok_rows - (tap_count - 1) :, :], "seq", 1)
    extended = jnp.concatenate([before, streams], axis=1).astype(jnp.float32)
    featured = jnp.zeros((3, tok_rows, chan_width), jnp.float32)
    for tap_index in range(tap_count):
        begin = tap_count - 1 - tap_index
        featured = (
            featured + short_taps[tap_index][:, None, :] * extended[:, begin : begin + tok_rows, :]
        )
    q_short = featured[0]
    k_short = featured[1]
    v_short = featured[2]
    gated = k_short * v_short
    mode_scale = residue * jnp.sqrt(-jnp.expm1(-2.0 * decay_rate))
    offsets = jnp.arange(tok_rows).astype(jnp.float32)
    shrink = jnp.exp(-decay_rate[None, :, :] * offsets[:, None, None])
    grow = jnp.exp(decay_rate[None, :, :] * offsets[:, None, None])
    scaled_shrink = mode_scale[None] * shrink
    scaled_grow = mode_scale[None] * grow
    one_step = jnp.exp(-decay_rate)
    block_decay = jnp.exp(-decay_rate * tok_rows)
    rows = jnp.arange(tok_rows)
    lower = (rows[:, None] >= rows[None, :]).astype(jnp.float32)
    upper = (rows[:, None] <= rows[None, :]).astype(jnp.float32)

    def prefix(tri, weights, signal):
        spread = (weights * signal[:, None, :]).reshape(tok_rows, mode_count * chan_width)
        summed = jnp.dot(tri, spread, precision=highest, preferred_element_type=jnp.float32)
        return summed.reshape(tok_rows, mode_count, chan_width)

    fwd_sums = prefix(lower, grow, gated)
    fwd_final = shrink[tok_rows - 1] * fwd_sums[tok_rows - 1]
    grad_mixer = lax.dot_general(
        grad_full, columns, (((1,), (1,)), ((), ())), preferred_element_type=jnp.float32
    )
    grad_long = grad_mixer * q_short
    bwd_sums = prefix(upper, shrink, grad_long)
    bwd_final = bwd_sums[0]
    finals = jnp.stack([fwd_final, bwd_final]).astype(jnp.bfloat16)
    gathered = lax.all_gather(finals, "seq").astype(jnp.float32)
    source = jnp.arange(count)
    fwd_gap = place - 1 - source
    bwd_gap = source - place - 1
    fwd_weight = jnp.where(
        (fwd_gap >= 0)[:, None, None],
        jnp.exp(
            -decay_rate[None]
            * (tok_rows * jnp.maximum(fwd_gap, 0)).astype(jnp.float32)[:, None, None]
        ),
        0.0,
    )
    bwd_weight = jnp.where(
        (bwd_gap >= 0)[:, None, None],
        jnp.exp(
            -decay_rate[None]
            * (tok_rows * jnp.maximum(bwd_gap, 0)).astype(jnp.float32)[:, None, None]
        ),
        0.0,
    )
    fwd_entry = jnp.sum(fwd_weight * gathered[:, 0], axis=0) * one_step
    bwd_entry = jnp.sum(bwd_weight * gathered[:, 1], axis=0) * block_decay
    long_out = (
        jnp.sum(scaled_shrink * (fwd_sums + fwd_entry[None]), axis=1) + skip_gain[None, :] * gated
    )
    mixer = (q_short * long_out).astype(jnp.bfloat16)
    partial_value = jnp.dot(mixer, columns, preferred_element_type=jnp.float32)
    mixed = lax.psum_scatter(
        partial_value.astype(jnp.bfloat16), "ch", scatter_dimension=1, tiled=True
    )
    grad_qshort = grad_mixer * long_out
    grad_gated = (
        jnp.sum(scaled_grow * (bwd_sums + bwd_entry[None]), axis=1) + skip_gain[None, :] * grad_long
    )
    grad_stack = jnp.stack([grad_qshort, grad_gated * v_short, grad_gated * k_short])
    after = from_behind(grad_stack[:, : tap_count - 1, :], "seq", -1)
    extended_back = jnp.concatenate([grad_stack, after], axis=1)
    grads = jnp.zeros((3, tok_rows, chan_width), jnp.float32)
    for tap_index in range(tap_count):
        grads = (
            grads
            + short_taps[tap_index][:, None, :]
            * extended_back[:, tap_index : tap_index + tok_rows, :]
        )
    grads = grads.astype(jnp.bfloat16)
    return (mixed, grads[0], grads[1], grads[2])


def solution(mesh):
    in_specs = (
        P("seq", "ch"),
        P("seq", "ch"),
        P("seq", "ch"),
        P(None, None, "ch"),
        P(None, "ch"),
        P(None, "ch"),
        P("ch"),
        P("ch", "seq"),
        P("seq", "ch"),
    )
    out_specs = (P("seq", "ch"), P("seq", "ch"), P("seq", "ch"), P("seq", "ch"))
    return jax.shard_map(
        per_device, mesh=mesh, in_specs=in_specs, out_specs=out_specs, check_vma=False
    )
```

profile of v0, /device:TPU:2, one launch (start us, length us, event | category | flops | bytes accessed | tf_op | source)
XLA Modules:
  0.0 272.1 jit_solution(8991568533417485764)
XLA Ops:
  7.3 0.7 all-gather.3.cloned.1.call-update
  8.0 0.7 all-gather.5.cloned.1.call-update
  8.7 0.7 pad_maximum_fusion.3
  9.5 1.7 collective-permute-start
  11.3 0.7 slice_bitcast_fusion.10
  12.0 0.8 fusion.32
  12.8 2.6 multiply_exponential_fusion
  15.6 0.2 fusion.19
  15.8 50.0 %all-gather.3.cloned.1.call-done = bf16[128,8192]{1,0:T(8,128)(2,1)} async-done(((bf16[128,512]{1,0:T(8,128)(2,1)}), bf16[128,8192]{1,0:T(8,128)(2,1)}) %all-gather.3.cloned.1.call-update) | async-done | bytes 2097168 | tf_op jit(solution)/shard_map/all_gather | solution.py:21
  65.8 57.5 %all-gather.5.cloned.1.call-done = bf16[512,8192]{1,0:T(8,128)(2,1)} async-done(((bf16[512,512]{1,0:T(8,128)(2,1)}), bf16[512,8192]{1,0:T(8,128)(2,1)}) %all-gather.5.cloned.1.call-update) | async-done | bytes 8388624 | tf_op jit(solution)/shard_map/all_gather | solution.py:20
  123.3 7.0 %fusion.26 = (f32[128,512]{1,0:T(8,128)S(1)}, f32[128,512]{1,0:T(8,128)S(1)}, f32[128,512]{1,0:T(8,128)S(1)}) fusion(f32[3,128,512]{2,1,0:T(8,128)S(1)} %fusion.19, bf16[128,8192]{1,0:T(8,128)(2,1)} %all-gather.3.cloned.1.call-done, bf16[512,8192]{1,0:T(8,128)(2,1)} %all-gather.5.cloned.1.call-done), kind=kOutput, calls=%fused_computation.49 | convolution fusion | flops 1073872896 | bytes 12058624 | tf_op jit(solution)/shard_map/dot_general | solution.py:54
  130.3 0.5 mul.273
  130.9 3.4 %copy.20 = f32[16,8,16,512]{3,1,2,0:T(8,128)S(1)} copy(f32[16,8,16,512]{3,2,1,0:T(8,128)S(1)} %bitcast.88) | data formatting | bytes 8388608
  134.3 3.0 %fusion.4 = f32[128,8192]{1,0:T(8,128)S(1)} fusion(f32[128,8192]{1,0:T(8,128)S(1)} %bitcast.86, f32[8192]{0:T(1024)S(1)} %bitcast.98, f32[128]{0:T(128)S(1)} %iota_convert_fusion), kind=kOutput, calls=%fused_computation.7 | convolution fusion | flops 1612726272 | bytes 8421888 | tf_op jit(solution)/shard_map/dot_general | solution.py:49
  137.3 1.9 copy-done
  139.4 7.5 %copy.21 = f32[16,8,16,512]{3,2,1,0:T(8,128)} copy(f32[16,8,16,512]{3,1,2,0:T(8,128)} %bitcast.84) | data formatting | bytes 8388608
  146.9 0.5 mul.261
  147.4 3.4 %copy.17 = f32[16,8,16,512]{3,1,2,0:T(8,128)S(1)} copy(f32[16,8,16,512]{3,2,1,0:T(8,128)S(1)} %bitcast.89) | data formatting | bytes 8388608
  150.9 3.0 %fusion.8 = f32[128,8192]{1,0:T(8,128)S(1)} fusion(f32[128,8192]{1,0:T(8,128)S(1)} %bitcast.87, f32[128]{0:T(128)S(1)} %iota_convert_fusion, f32[8192]{0:T(1024)S(1)} %bitcast.97), kind=kOutput, calls=%fused_computation.11 | convolution fusion | flops 1612726272 | bytes 8421888 | tf_op jit(solution)/shard_map/dot_general | solution.py:49
  153.9 1.9 copy-done.1
  156.0 5.6 %copy.18 = f32[16,8,16,512]{3,2,1,0:T(8,128)S(1)} copy(f32[16,8,16,512]{3,1,2,0:T(8,128)} %bitcast.85) | data formatting | bytes 8388608
  161.6 0.8 fusion.29
  162.4 17.1 %all_gather.12 = bf16[16,2,16,512]{3,2,1,0:T(8,128)(2,1)S(1)} all-gather(bf16[1,2,16,512]{3,2,1,0:T(8,128)(2,1)S(1)} %pad_maximum_fusion.2), channel_id=1, replica_groups=mesh['seq'=16,'ch'=16] {'seq'}, dimensions={0}, use_global_device_ids=true | all-gather | bytes 557056 | tf_op jit(solution)/shard_map/all_gather | solution.py:61
  179.7 0.3 fusion.22
  180.1 3.8 %fusion.1 = (f32[128,512]{1,0:T(8,128)S(1)}, f32[128,512]{1,0:T(8,128)S(1)}) fusion(f32[16,8,16,512]{3,2,1,0:T(8,128)S(1)} %copy-done.2, f32[16,512]{1,0:T(8,128)S(1)} %get-tuple-element.16, f32[16,512]{1,0:T(8,128)S(1)} %copy-done.3, f32[128]{0:T(128)S(1)} %iota_convert_fusion, f32[16,512]{1,0:T(8,128)S(1)} %get-tuple-element.17, ...), kind=kLoop, calls=%fused_computation.3 | loop fusion | flops 10354688 | bytes 9077248 | tf_op jit(solution)/shard_map/reduce_sum | solution.py:93
  183.9 2.6 convolution_convert_fusion
  186.5 0.2 multiply_bitcast_fusion.1
  186.8 1.3 collective-permute-start.1
  188.1 1.8 collective-permute-done.1
  190.0 0.3 fusion.17
  190.2 0.8 slice_bitcast_fusion.5
  191.0 74.6 %reduce-scatter.2.cloned.1.call-done = bf16[128,512]{1,0:T(8,128)(2,1)} async-done(((bf16[128,8192]{1,0:T(8,128)(2,1)}), bf16[128,512]{1,0:T(8,128)(2,1)}) %reduce-scatter.2.cloned.1.call-update) | async-done | bytes 131088 | tf_op jit(solution)/shard_map/reduce_scatter | solution.py:88
  (42 shorter events, 0.8 us)
Async XLA Ops:
  7.2 8.2 %copy-start.4 = (bf16[128,512]{1,0:T(8,128)(2,1)S(1)}, bf16[128,512]{1,0:T(8,128)(2,1)}, u32[]{:S(2)}) copy-start(bf16[128,512]{1,0:T(8,128)(2,1)} %param.11) | copy-start | bytes 393220
  7.2 8.2 %copy-start.5 = (bf16[128,512]{1,0:T(8,128)(2,1)S(1)}, bf16[128,512]{1,0:T(8,128)(2,1)}, u32[]{:S(2)}) copy-start(bf16[128,512]{1,0:T(8,128)(2,1)} %param.10) | copy-start | bytes 393220
  7.2 8.2 %copy-start.6 = (bf16[128,512]{1,0:T(8,128)(2,1)S(1)}, bf16[128,512]{1,0:T(8,128)(2,1)}, u32[]{:S(2)}) copy-start(bf16[128,512]{1,0:T(8,128)(2,1)} %param.9) | copy-start | bytes 393220
  7.2 8.2 %copy-start.3 = (f32[16,512]{1,0:T(8,128)S(1)}, f32[16,512]{1,0:T(8,128)}, u32[]{:S(2)}) copy-start(f32[16,512]{1,0:T(8,128)} %param.13) | copy-start | bytes 98308
  7.2 58.6 %all-gather.3.cloned.1.call-start = ((), (), s32[]{:S(2)}) async-start(), calls=%async_computation.1 | async-start | bytes 2228224 | tf_op jit(solution)/shard_map/all_gather | solution.py:21
  7.9 115.4 %all-gather.5.cloned.1.call-start = ((), (), s32[]{:S(2)}) async-start(), calls=%async_computation.2 | async-start | bytes 8912896 | tf_op jit(solution)/shard_map/all_gather | solution.py:20
  8.7 256.9 %reduce-scatter.2.cloned.1.call-start = ((), (), s32[]{:S(2)}) async-start(), calls=%async_computation.3 | async-start | bytes 2228224 | tf_op jit(solution)/shard_map/reduce_scatter | solution.py:88
  9.5 5.9 %collective-permute-start = (bf16[3,2,512]{2,1,0:T(2,128)(2,1)S(1)}, bf16[3,2,512]{2,1,0:T(2,128)(2,1)S(1)}, u32[]{:S(2)}, u32[]{:S(2)}) collective-permute-start(bf16[3,2,512]{2,1,0:T(2,128)(2,1)S(1)} %pad_maximum_fusion.3), channel_id=1, source_target_pairs={{0,16},{16,32},{32,48},{48,64},{64,80},{80,96},{96,112},{112,128},... | collective-permute-start | bytes 18440 | tf_op jit(solution)/shard_map/ppermute | solution.py:10
  137.3 1.9 copy-start
  153.9 1.9 copy-start.1
  155.9 24.0 %copy-start.8 = (f32[16,512]{1,0:T(8,128)S(1)}, f32[16,512]{1,0:T(8,128)}, u32[]{:S(2)}) copy-start(f32[16,512]{1,0:T(8,128)} %param.14) | copy-start | bytes 98308
  155.9 24.1 %copy-start.2 = (f32[16,8,16,512]{3,2,1,0:T(8,128)S(1)}, f32[16,8,16,512]{3,2,1,0:T(8,128)}, u32[]{:S(2)}) copy-start(f32[16,8,16,512]{3,2,1,0:T(8,128)} %copy.21) | copy-start | bytes 12582916
  155.9 27.9 %slice-start = ((s8[8388608]{0:T(1024)(128)(4,1)}), s8[4194304]{0:T(1024)(128)(4,1)S(1)}, s32[]{:S(2)}) async-start(s8[8388608]{0:T(1024)(128)(4,1)} %bitcast.82), calls=%async_computation.4 | async-start | bytes 8388608
  179.5 4.4 %slice-start.1 = ((s8[8388608]{0:T(1024)(128)(4,1)}), s8[4194304]{0:T(1024)(128)(4,1)S(1)}, s32[]{:S(2)}) async-start(s8[8388608]{0:T(1024)(128)(4,1)} %bitcast.82), calls=%async_computation.5 | async-start | bytes 8388608
  180.0 3.9 %copy-start.7 = (f32[512]{0:T(512)S(1)}, f32[512]{0:T(512)}, u32[]{:S(2)}) copy-start(f32[512]{0:T(512)} %param.15) | copy-start | bytes 6148
  186.8 3.1 %collective-permute-start.1 = (f32[3,2,512]{2,1,0:T(2,128)S(1)}, f32[3,2,512]{2,1,0:T(2,128)S(1)}, u32[]{:S(2)}, u32[]{:S(2)}) collective-permute-start(f32[3,2,512]{2,1,0:T(2,128)S(1)} %slice.101), channel_id=1, source_target_pairs={{16,0},{32,16},{48,32},{64,48},{80,64},{96,80},{112,96},{128,112},... | collective-permute-start | bytes 36872 | tf_op jit(solution)/shard_map/ppermute | solution.py:10
Sparse Core Ops, SparseCore 0:
  10.4 55.3 all-gather.2
  67.6 55.6 all-gather.4
  186.7 78.8 reduce-scatter.1
where the time goes:
time: 272 us
  waiting for transfers between devices  185 us (68%)
  local copies, waits for them, and re-layouts  26.7 us (10%)
  blocking collectives  17.1 us (6%)
  matrix products  15.6 us (6%)
  between operations  14.1 us (5%)
  other arithmetic  10.1 us (4%)
  starting transfers between devices  3.14 us (1%)
    reduce_scatter x1, waiting for transfers between devices, per_device(): lax.psum_scatter(partial_value.astype(jnp.bfloat16), 'ch', scatter_dimens...  74.6 us
    all_gather x1, waiting for transfers between devices, per_device(): columns = lax.all_gather(out_weight, 'seq', axis=1, tiled=True)  57.5 us
    all_gather x1, waiting for transfers between devices, per_device(): grad_full = lax.all_gather(grad_out, 'ch', axis=1, tiled=True)  50 us
    unnamed x28, local copies, waits for them, and re-layouts  24 us
    all_gather x1, blocking collectives, per_device(): gathered = lax.all_gather(finals, 'seq').astype(jnp.float32)  17.1 us
    dot_general x1, matrix products, per_device(): lax.dot_general(grad_full, columns, (((1,), (1,)), ((), ())), preferred_e...  6.97 us
    dot_general x2, matrix products, prefix(): jnp.dot(tri, spread, precision=highest, preferred_element_type=jnp.float32)  6.02 us
  transfers between devices with their start and end apart: 5, of which 4 were waited for; matrix products, arithmetic and copies ran while one was open for 2% of the time, Pallas kernels for 0%

commit v1 on v0

--- a/solution.py
+++ b/solution.py
@@ -18,7 +18,9 @@
     count = lax.axis_size("seq")
     place = lax.axis_index("seq")
     columns = lax.all_gather(out_weight, "seq", axis=1, tiled=True)
-    grad_full = lax.all_gather(grad_out, "ch", axis=1, tiled=True)
+    grad_full = jnp.concatenate(
+        lax.all_to_all(jnp.stack([grad_out] * lax.axis_size("ch")), "ch", 0, 0), axis=1
+    )
     streams = jnp.stack([query, key, value])
     before = from_behind(streams[:, tok_rows - (tap_count - 1) :, :], "seq", 1)
     extended = jnp.concatenate([before, streams], axis=1).astype(jnp.float32)

time: 272 us -> 218 us (0.80)
  waiting for transfers between devices: 185 us -> 122 us
  starting transfers between devices: 3.14 us -> 10.1 us
    all_gather x1 -> x0, waiting for transfers between devices: 50 us -> none  [per_device(): grad_full = lax.all_gather(grad_out, 'ch', axis=1, tiled=True)]
    all_gather x1, waiting for transfers between devices: 57.5 us -> 23.5 us  [per_device(): columns = lax.all_gather(out_weight, 'seq', axis=1, tiled=True)]
    all_to_all x0 -> x1, waiting for transfers between devices: none -> 21.5 us  [per_device(): lax.all_to_all(jnp.stack([grad_out] * lax.axis_size('ch')), 'ch', 0, 0)]
    all_to_all x0 -> x1, starting transfers between devices: none -> 7.48 us  [per_device(): lax.all_to_all(jnp.stack([grad_out] * lax.axis_size('ch')), 'ch', 0, 0)]
    unnamed x28 -> x49, local copies, waits for them, and re-layouts: 24 us -> 25 us
  transfers between devices with their start and end apart: 5 -> 5, of which waited for: 4 -> 4; matrix products, arithmetic and copies ran while one was open for 2% -> 4% of each run, Pallas kernels for 0% -> 0%
where the time goes in v1:
time: 218 us
  waiting for transfers between devices  122 us (56%)
  local copies, waits for them, and re-layouts  28.8 us (13%)
  blocking collectives  17.1 us (8%)
  matrix products  15.6 us (7%)
  between operations  14.6 us (7%)
  starting transfers between devices  10.1 us (5%)
  other arithmetic  9.71 us (4%)
    reduce_scatter x1, waiting for transfers between devices, per_device(): lax.psum_scatter(partial_value.astype(jnp.bfloat16), 'ch', scatter_dimens...  74.5 us
    unnamed x49, local copies, waits for them, and re-layouts  25 us
    all_gather x1, waiting for transfers between devices, per_device(): columns = lax.all_gather(out_weight, 'seq', axis=1, tiled=True)  23.5 us
    all_to_all x1, waiting for transfers between devices, per_device(): lax.all_to_all(jnp.stack([grad_out] * lax.axis_size('ch')), 'ch', 0, 0)  21.5 us
    all_gather x1, blocking collectives, per_device(): gathered = lax.all_gather(finals, 'seq').astype(jnp.float32)  17.1 us
    all_to_all x1, starting transfers between devices, per_device(): lax.all_to_all(jnp.stack([grad_out] * lax.axis_size('ch')), 'ch', 0, 0)  7.48 us
    dot_general x1, matrix products, per_device(): lax.dot_general(grad_full, columns, (((1,), (1,)), ((), ())), preferred_e...  7.01 us
    dot_general x2, matrix products, prefix(): jnp.dot(tri, spread, precision=highest, preferred_element_type=jnp.float32)  6.02 us
  transfers between devices with their start and end apart: 5, of which 4 were waited for; matrix products, arithmetic and copies ran while one was open for 4% of the time, Pallas kernels for 0%

profile of v1, /device:TPU:2, one launch (start us, length us, event | category | flops | bytes accessed | tf_op | source)
XLA Modules:
  0.0 218.0 jit_solution(8251444284375878676)
XLA Ops:
  7.3 0.7 all-gather.2.cloned.1.call-update
  8.0 1.0 copy.16
  9.0 1.7 stack.56
  10.7 7.5 %all-to-all-start = ((bf16[16,128,512]{1,2,0:T(8,128)(2,1)}), bf16[16,128,512]{1,2,0:T(8,128)(2,1)S(1)}, u32[]{:S(2)}, u32[]{:S(2)}) async-start(bf16[16,128,512]{1,2,0:T(8,128)(2,1)} %stack.56), calls=%async_computation | async-start | bytes 4194304 | tf_op jit(solution)/shard_map/all_to_all | solution.py:22
  18.3 1.3 collective-permute-start
  19.6 0.5 multiply_convert_fusion.2
  20.2 2.6 %multiply_exponential_fusion = f32[128,16,512]{2,1,0:T(8,128)} fusion(f32[128]{0:T(128)S(1)} %iota_convert_fusion, f32[16,512]{1,0:T(8,128)S(1)} %get-tuple-element.18), kind=kLoop, calls=%fused_computation.15 | loop fusion | flops 1048576 | bytes 4227584 | tf_op jit(solution)/shard_map/exp | solution.py:39
  22.8 0.6 fusion.30
  23.5 0.2 fusion.19
  23.8 21.5 %all-to-all-done = bf16[16,128,512]{1,2,0:T(8,128)(2,1)S(1)} async-done(((bf16[16,128,512]{1,2,0:T(8,128)(2,1)}), bf16[16,128,512]{1,2,0:T(8,128)(2,1)S(1)}, u32[]{:S(2)}, u32[]{:S(2)}) %all-to-all-start) | async-done | bytes 2097184 | tf_op jit(solution)/shard_map/all_to_all | solution.py:22
  45.3 23.5 %all-gather.2.cloned.1.call-done = bf16[512,8192]{1,0:T(8,128)(2,1)} async-done(((bf16[512,512]{1,0:T(8,128)(2,1)}), bf16[512,8192]{1,0:T(8,128)(2,1)}) %all-gather.2.cloned.1.call-update) | async-done | bytes 8388624 | tf_op jit(solution)/shard_map/all_gather | solution.py:20
  68.8 7.0 %fusion.26 = (f32[128,512]{1,0:T(8,128)S(1)}, f32[128,512]{1,0:T(8,128)S(1)}, f32[128,512]{1,0:T(8,128)}) fusion(f32[3,128,512]{2,1,0:T(8,128)S(1)} %fusion.19, bf16[128,8192]{0,1:T(8,128)(2,1)S(1)} %bitcast.93, bf16[512,8192]{1,0:T(8,128)(2,1)} %all-gather.2.cloned.1.call-done), kind=kOutput, calls=%fused_computation.49 | convolution fusion | flops 1073872896 | bytes 12058624 | tf_op jit(solution)/shard_map/dot_general | solution.py:56
  75.8 0.5 mul.273
  76.4 3.4 %copy.23 = f32[16,8,16,512]{3,1,2,0:T(8,128)S(1)} copy(f32[16,8,16,512]{3,2,1,0:T(8,128)S(1)} %bitcast.91) | data formatting | bytes 8388608
  79.8 3.0 %fusion.4 = f32[128,8192]{1,0:T(8,128)S(1)} fusion(f32[128,8192]{1,0:T(8,128)S(1)} %bitcast.89, f32[8192]{0:T(1024)S(1)} %bitcast.102, f32[128]{0:T(128)S(1)} %copy-done.14), kind=kOutput, calls=%fused_computation.7 | convolution fusion | flops 1612726272 | bytes 8421888 | tf_op jit(solution)/shard_map/dot_general | solution.py:51
  82.8 1.9 copy-done
  84.9 7.6 %copy.24 = f32[16,8,16,512]{3,2,1,0:T(8,128)} copy(f32[16,8,16,512]{3,1,2,0:T(8,128)} %bitcast.87) | data formatting | bytes 8388608
  92.4 0.5 mul.261
  93.0 3.4 %copy.20 = f32[16,8,16,512]{3,1,2,0:T(8,128)S(1)} copy(f32[16,8,16,512]{3,2,1,0:T(8,128)S(1)} %bitcast.92) | data formatting | bytes 8388608
  96.4 3.0 %fusion.8 = f32[128,8192]{1,0:T(8,128)S(1)} fusion(f32[128,8192]{1,0:T(8,128)S(1)} %bitcast.90, f32[128]{0:T(128)S(1)} %copy-done.14, f32[8192]{0:T(1024)S(1)} %bitcast.101), kind=kOutput, calls=%fused_computation.11 | convolution fusion | flops 1612726272 | bytes 8421888 | tf_op jit(solution)/shard_map/dot_general | solution.py:51
  99.4 1.9 copy-done.1
  101.5 5.6 %copy.21 = f32[16,8,16,512]{3,2,1,0:T(8,128)S(1)} copy(f32[16,8,16,512]{3,1,2,0:T(8,128)} %bitcast.88) | data formatting | bytes 8388608
  107.2 0.8 fusion.29
  107.9 17.1 %all_gather.8 = bf16[16,2,16,512]{3,2,1,0:T(8,128)(2,1)S(1)} all-gather(bf16[1,2,16,512]{3,2,1,0:T(8,128)(2,1)S(1)} %pad_maximum_fusion.2), channel_id=1, replica_groups=mesh['seq'=16,'ch'=16] {'seq'}, dimensions={0}, use_global_device_ids=true | all-gather | bytes 557056 | tf_op jit(solution)/shard_map/all_gather | solution.py:63
  125.2 0.3 fusion.22
  125.6 3.8 %fusion.1 = (f32[128,512]{1,0:T(8,128)S(1)}, f32[128,512]{1,0:T(8,128)S(1)}) fusion(f32[16,8,16,512]{3,2,1,0:T(8,128)S(1)} %copy-done.2, f32[16,512]{1,0:T(8,128)S(1)} %get-tuple-element.16, f32[16,512]{1,0:T(8,128)S(1)} %copy-done.4, f32[128]{0:T(128)S(1)} %copy-done.14, f32[16,512]{1,0:T(8,128)S(1)} %get-tuple-element.17, ...), kind=kLoop, calls=%fused_computation.3 | loop fusion | flops 10354688 | bytes 9077248 | tf_op jit(solution)/shard_map/reduce_sum | solution.py:95
  129.5 2.6 %convolution_convert_fusion = bf16[128,8192]{1,0:T(8,128)(2,1)} fusion(bf16[512,8192]{1,0:T(8,128)(2,1)S(1)} %bitcast.86, f32[3,128,512]{2,1,0:T(8,128)S(1)} %fusion.19, f32[128,512]{1,0:T(8,128)S(1)} %get-tuple-element.7, f32[128,512]{1,0:T(8,128)S(1)} %get-tuple-element.10, f32[512]{0:T(512)S(1)} %copy-done.10), kind=kOutput, calls=%fused_computation | convolution fusion | flops 1075052544 | bytes 11274240 | tf_op jit(solution)/shard_map/dot_general | solution.py:89
  132.4 1.3 collective-permute-start.1
  133.7 1.8 collective-permute-done.1
  135.6 0.3 fusion.17
  135.8 0.8 slice_bitcast_fusion.5
  136.6 74.5 %reduce-scatter.2.cloned.1.call-done = bf16[128,512]{1,0:T(8,128)(2,1)} async-done(((bf16[128,8192]{1,0:T(8,128)(2,1)}), bf16[128,512]{1,0:T(8,128)(2,1)}) %reduce-scatter.2.cloned.1.call-update) | async-done | bytes 131088 | tf_op jit(solution)/shard_map/reduce_scatter | solution.py:90
  (63 shorter events, 1.0 us)
Async XLA Ops:
  7.2 11.1 %copy-start.5 = (bf16[128,512]{1,0:T(8,128)(2,1)S(1)}, bf16[128,512]{1,0:T(8,128)(2,1)}, u32[]{:S(2)}) copy-start(bf16[128,512]{1,0:T(8,128)(2,1)} %param.11) | copy-start | bytes 393220
  7.2 11.1 %copy-start.6 = (bf16[128,512]{1,0:T(8,128)(2,1)S(1)}, bf16[128,512]{1,0:T(8,128)(2,1)}, u32[]{:S(2)}) copy-start(bf16[128,512]{1,0:T(8,128)(2,1)} %param.10) | copy-start | bytes 393220
  7.2 11.1 %copy-start.7 = (bf16[128,512]{1,0:T(8,128)(2,1)S(1)}, bf16[128,512]{1,0:T(8,128)(2,1)}, u32[]{:S(2)}) copy-start(bf16[128,512]{1,0:T(8,128)(2,1)} %param.9) | copy-start | bytes 393220
  7.2 12.9 %copy-start.12 = (f32[3,3,512]{2,1,0:T(4,128)S(1)}, f32[3,3,512]{2,1,0:T(4,128)}, u32[]{:S(2)}) copy-start(f32[3,3,512]{2,1,0:T(4,128)} %param.12) | copy-start | bytes 55300
  7.2 12.9 %copy-start.4 = (f32[16,512]{1,0:T(8,128)S(1)}, f32[16,512]{1,0:T(8,128)}, u32[]{:S(2)}) copy-start(f32[16,512]{1,0:T(8,128)} %param.13) | copy-start | bytes 98308
  7.2 61.6 %all-gather.2.cloned.1.call-start = ((), (), s32[]{:S(2)}) async-start(), calls=%async_computation.2 | async-start | bytes 8912896 | tf_op jit(solution)/shard_map/all_gather | solution.py:20
  10.7 34.6 %all-to-all-start = ((bf16[16,128,512]{1,2,0:T(8,128)(2,1)}), bf16[16,128,512]{1,2,0:T(8,128)(2,1)S(1)}, u32[]{:S(2)}, u32[]{:S(2)}) async-start(bf16[16,128,512]{1,2,0:T(8,128)(2,1)} %stack.56), calls=%async_computation | async-start | bytes 4194304 | tf_op jit(solution)/shard_map/all_to_all | solution.py:22
  18.2 193.0 %reduce-scatter.2.cloned.1.call-start = ((), (), s32[]{:S(2)}) async-start(), calls=%async_computation.3 | async-start | bytes 2228224 | tf_op jit(solution)/shard_map/reduce_scatter | solution.py:90
  18.3 5.1 %collective-permute-start = (bf16[3,2,512]{2,1,0:T(2,128)(2,1)S(1)}, bf16[3,2,512]{2,1,0:T(2,128)(2,1)S(1)}, u32[]{:S(2)}, u32[]{:S(2)}) collective-permute-start(bf16[3,2,512]{2,1,0:T(2,128)(2,1)S(1)} %pad_maximum_fusion.3), channel_id=1, source_target_pairs={{0,16},{16,32},{32,48},{48,64},{64,80},{80,96},{96,112},{112,128},... | collective-permute-start | bytes 18440 | tf_op jit(solution)/shard_map/ppermute | solution.py:10
  19.6 3.8 %copy-start.13 = (f32[128]{0:T(128)}, f32[128]{0:T(128)S(1)}, u32[]{:S(2)}) copy-start(f32[128]{0:T(128)S(1)} %iota_convert_fusion) | copy-start | bytes 1540
  20.2 3.6 %copy-start.8 = (f32[3,512]{1,0:T(4,128)}, f32[3,512]{1,0:T(4,128)S(1)}, u32[]{:S(2)}) copy-start(f32[3,512]{1,0:T(4,128)S(1)} %get-tuple-element.22) | copy-start | bytes 18436
  76.3 3.4 %copy-start.14 = (f32[128]{0:T(128)S(1)}, f32[128]{0:T(128)}, u32[]{:S(2)}) copy-start(f32[128]{0:T(128)} %copy-done.13) | copy-start | bytes 1540
  82.8 1.9 copy-start
  99.4 1.9 copy-start.1
  101.4 23.8 %copy-start.15 = (f32[16]{0:T(128)S(1)}, f32[16]{0:T(128)}, u32[]{:S(2)}) copy-start(f32[16]{0:T(128)} %get-tuple-element.25) | copy-start | bytes 196
  101.4 23.8 %copy-start.16 = (f32[16]{0:T(128)S(1)}, f32[16]{0:T(128)}, u32[]{:S(2)}) copy-start(f32[16]{0:T(128)} %get-tuple-element.26) | copy-start | bytes 196
  101.5 23.8 %copy-start.17 = (pred[16]{0:T(512)(128)(4,1)S(1)}, pred[16]{0:T(512)(128)(4,1)}, u32[]{:S(2)}) copy-start(pred[16]{0:T(512)(128)(4,1)} %get-tuple-element.27) | copy-start | bytes 52
  101.5 23.8 %copy-start.18 = (pred[16]{0:T(512)(128)(4,1)S(1)}, pred[16]{0:T(512)(128)(4,1)}, u32[]{:S(2)}) copy-start(pred[16]{0:T(512)(128)(4,1)} %get-tuple-element.28) | copy-start | bytes 52
  101.5 24.1 %copy-start.11 = (f32[16,512]{1,0:T(8,128)S(1)}, f32[16,512]{1,0:T(8,128)}, u32[]{:S(2)}) copy-start(f32[16,512]{1,0:T(8,128)} %param.14) | copy-start | bytes 98308
  101.5 24.1 %copy-start.2 = (f32[16,8,16,512]{3,2,1,0:T(8,128)S(1)}, f32[16,8,16,512]{3,2,1,0:T(8,128)}, u32[]{:S(2)}) copy-start(f32[16,8,16,512]{3,2,1,0:T(8,128)} %copy.24) | copy-start | bytes 12582916
  101.5 27.9 %slice-start = ((s8[8388608]{0:T(1024)(128)(4,1)}), s8[4194304]{0:T(1024)(128)(4,1)S(1)}, s32[]{:S(2)}) async-start(s8[8388608]{0:T(1024)(128)(4,1)} %bitcast.85), calls=%async_computation.4 | async-start | bytes 8388608
  125.1 4.4 %slice-start.1 = ((s8[8388608]{0:T(1024)(128)(4,1)}), s8[4194304]{0:T(1024)(128)(4,1)S(1)}, s32[]{:S(2)}) async-start(s8[8388608]{0:T(1024)(128)(4,1)} %bitcast.85), calls=%async_computation.5 | async-start | bytes 8388608
  125.6 3.8 %copy-start.10 = (f32[512]{0:T(512)S(1)}, f32[512]{0:T(512)}, u32[]{:S(2)}) copy-start(f32[512]{0:T(512)} %param.15) | copy-start | bytes 6148
  129.5 2.6 %copy-start.3 = (f32[128,512]{1,0:T(8,128)S(1)}, f32[128,512]{1,0:T(8,128)}, u32[]{:S(2)}) copy-start(f32[128,512]{1,0:T(8,128)} %get-tuple-element.24) | copy-start | bytes 786436
  132.1 3.5 %copy-start.9 = (f32[3,512]{1,0:T(4,128)S(1)}, f32[3,512]{1,0:T(4,128)}, u32[]{:S(2)}) copy-start(f32[3,512]{1,0:T(4,128)} %copy-done.8) | copy-start | bytes 18436
  132.4 3.1 %collective-permute-start.1 = (f32[3,2,512]{2,1,0:T(2,128)S(1)}, f32[3,2,512]{2,1,0:T(2,128)S(1)}, u32[]{:S(2)}, u32[]{:S(2)}) collective-permute-start(f32[3,2,512]{2,1,0:T(2,128)S(1)} %slice.101), channel_id=1, source_target_pairs={{16,0},{32,16},{48,32},{64,48},{80,64},{96,80},{112,96},{128,112},... | collective-permute-start | bytes 36872 | tf_op jit(solution)/shard_map/ppermute | solution.py:10
Sparse Core Ops, SparseCore 0:
  9.9 58.8 all-gather.1
  132.3 78.8 reduce-scatter.1
